TPU v7x, 32 devices: a whole 2x2x4 slice. The times are simulated.
32 devices in a mesh: chan: 16 (over z, x, core), tm: 2 (over y).
Axes of the slice: x: 2, y: 2, z: 4, core: 2. Of those that a mesh axis runs over, the one named last changes fastest.
Arguments:
- samples: bfloat16 [96, 2, 2048], P('chan', 'tm'), may hold values from -6 to 6
- dead_flags: int32 [96], P('chan'), may hold values 0 or 1
- pair_mask: int32 [96, 96], P('chan', 'tm'), may hold values 0 or 1
Outputs:
- xcorr: float32 [96, 96, 301], P('chan', 'tm')
All inputs are finite; a program needn't handle non-finite values. No bound on the sum of `dead_flags` or of `pair_mask` on one device may be relied on, other than what follows from the above.
Results may differ from a plain program's by a relative error of at most 0.0095.
Values may be sent and summed in bfloat16 or wider, within the bound.
A program may use at most 64 MiB of HBM per device.

v0:
```python
import math
import jax
import jax.numpy as jnp
from jax import lax
from jax.sharding import PartitionSpec as P

F = 768
LAGS = 301


def taper_window(length):
    sample_index = jnp.arange(length, dtype=jnp.float32)
    return 0.5 - 0.5 * jnp.cos(2.0 * math.pi * (sample_index + 0.5) / length)


def forward_table(length, bins):
    sample_index = jnp.arange(length, dtype=jnp.int32)
    frequency = jnp.arange(1, bins + 1, dtype=jnp.int32)
    phase_index = sample_index[:, None] * frequency[None, :] % length
    angles = 2.0 * math.pi / length * phase_index.astype(jnp.float32)
    return jnp.concatenate([jnp.cos(angles), -jnp.sin(angles)], axis=1).astype(jnp.bfloat16)


def lag_table(length, bins, lags, factor):
    frequency = jnp.arange(1, bins + 1, dtype=jnp.int32)
    shifts = jnp.arange(lags, dtype=jnp.int32) - (lags - 1) // 2
    phase_index = jnp.mod(frequency[:, None] * shifts[None, :], length)
    angles = 2.0 * math.pi / length * phase_index.astype(jnp.float32)
    table_values = jnp.concatenate([jnp.cos(angles), -jnp.sin(angles)], axis=0) * factor
    return table_values.astype(jnp.bfloat16)


def whiten(samples, dead_flags, table_values):
    channel_count, windows, length = samples.shape
    bins = table_values.shape[1] // 2
    traces = samples.astype(jnp.float32)
    traces = traces - jnp.mean(traces, axis=-1, keepdims=True)
    tapered = (traces * taper_window(length)).astype(jnp.bfloat16)
    spectra = jnp.dot(
        tapered.reshape(channel_count * windows, length),
        table_values,
        preferred_element_type=jnp.float32,
    )
    real_part = spectra[:, :bins]
    imag_part = spectra[:, bins:]
    energy = real_part * real_part + imag_part * imag_part
    mean_energy = jnp.mean(energy, axis=-1, keepdims=True)
    inverse_scale = lax.rsqrt(energy + 0.25 * mean_energy + 1e-06)
    alive_rows = jnp.repeat((1 - dead_flags).astype(jnp.float32), windows)[:, None]
    whitened = (
        jnp.concatenate([real_part * inverse_scale, imag_part * inverse_scale], axis=1) * alive_rows
    )
    return whitened.astype(jnp.bfloat16).reshape(channel_count, windows, 2 * bins)


def correlate(receivers, sources, lag_weights):
    bins = receivers.shape[-1] // 2
    rec_values = receivers.astype(jnp.float32)
    src_values = sources.astype(jnp.float32)
    rec_re = rec_values[:, None, :, :bins]
    rec_im = rec_values[:, None, :, bins:]
    src_re = src_values[None, :, :, :bins]
    src_im = src_values[None, :, :, bins:]
    cross_re = rec_re * src_re + rec_im * src_im
    cross_im = rec_im * src_re - rec_re * src_im
    cross = jnp.concatenate([cross_re, cross_im], axis=-1).astype(jnp.bfloat16)
    result = jnp.einsum("rgwk,kl->wrgl", cross, lag_weights, preferred_element_type=jnp.float32)
    return result.astype(jnp.bfloat16)


def pick_group(source_count, rows_each):
    chosen = 1
    for candidate in range(1, source_count + 1):
        if source_count % candidate == 0 and candidate * rows_each <= 1024:
            chosen = candidate
    return chosen


def per_device(samples, dead_flags, pair_mask):
    block_size, local_windows, length = samples.shape
    table_values = forward_table(length, F)
    whitened = whiten(samples, dead_flags, table_values)
    subwin = local_windows * lax.axis_size("tm")
    lag_weights = lag_table(length, F, LAGS, 1.0 / math.sqrt(subwin * F))
    incoming = lax.all_gather(whitened, "chan", axis=0, tiled=True)
    source_count = incoming.shape[0]
    group_size = pick_group(source_count, block_size * local_windows)
    grouped = incoming.reshape(source_count // group_size, group_size, local_windows, 2 * F)

    def one_group(group_sources):
        return correlate(whitened, group_sources, lag_weights)[0]

    results = lax.map(one_group, grouped)
    placed = jnp.transpose(results, (1, 0, 2, 3)).reshape(block_size, source_count, LAGS)
    shares = lax.psum_scatter(
        placed.astype(jnp.float32).astype(jnp.bfloat16), "tm", scatter_dimension=1, tiled=True
    ).astype(jnp.float32)
    return shares * pair_mask.astype(jnp.float32)[..., None]


def solution(mesh):
    in_specs = (P("chan", "tm", None), P("chan"), P("chan", "tm"))
    out_specs = P("chan", "tm", None)
    return jax.shard_map(
        per_device, mesh=mesh, in_specs=in_specs, out_specs=out_specs, check_vma=False
    )
```

profile of v0, /device:TPU:0, one launch (start us, length us, event | category | flops | bytes accessed | tf_op | source)
XLA Modules:
  0.0 85.0 jit_solution(8352473777845611654)
XLA Ops:
  6.5 0.0 reduce-scatter.2.cloned.1.call-start
  6.5 0.1 multiply_subtract_fusion
  6.6 0.0 copy-start
  6.6 25.4 %cosine_convert_fusion = (bf16[2048,768]{1,0:T(8,128)(2,1)S(1)}, bf16[2048,768]{1,0:T(8,128)(2,1)S(1)}) fusion(s32[768]{0:T(1024)S(1)} %iota_add_fusion), kind=kLoop, calls=%fused_computation.11 | loop fusion | flops 26738688 | bytes 6294528 | tf_op jit(solution)/shard_map/convert.2
  32.1 0.0 copy-done
  32.1 0.1 convert_reduce_fusion
  32.2 0.0 copy-start.2
  32.2 1.0 %fusion.3 = f32[6,1536]{1,0:T(8,128)S(1)} fusion(bf16[2048,768]{1,0:T(8,128)(2,1)S(1)} %get-tuple-element.33, bf16[2048,768]{1,0:T(8,128)(2,1)S(1)} %get-tuple-element.32, bf16[6,1,2048]{2,0,1:T(8,128)(2,1)S(1)} %copy-done, f32[2048]{0:T(1024)S(1)} %multiply_subtract_fusion, f32[6]{0:T(128)S(1)} %broadcast_multiply_fusion.1), kind=kOutput, calls=%fused_computation.6 | convolution fusion | flops 50380800 | bytes 6361112 | tf_op jit(solution)/shard_map/dot_general | solution.py:39
  33.2 0.1 fusion.39
  33.3 0.1 multiply_bitcast_fusion.1
  33.4 0.0 copy-done.2
  33.4 0.1 fusion.40
  33.5 24.9 %all_gather.3 = bf16[96,1,1536]{2,1,0:T(2,128)(2,1)S(1)} all-gather(bf16[6,1,1536]{2,1,0:T(2,128)(2,1)S(1)} %copy.4), channel_id=1, replica_groups=mesh['chan'=16,'tm'=2] {'chan'}, dimensions={0}, use_global_device_ids=true | all-gather | bytes 313344 | tf_op jit(solution)/shard_map/all_gather | solution.py:85
  58.4 0.6 fusion.42
  59.0 3.7 %fusion.27 = (f32[768,301]{0,1:T(8,128)S(1)}, f32[768,301]{0,1:T(8,128)S(1)}) fusion(s32[301]{0:T(512)S(1)} %iota_add_fusion.1, s32[768]{0:T(1024)S(1)} %iota_add_fusion), kind=kLoop, calls=%fused_computation.36 | loop fusion | flops 3467520 | bytes 1853620 | tf_op jit(solution)/shard_map/cos | solution.py:29
  62.8 0.5 add_convert_fusion
  63.3 0.0 copy-start.1
  63.3 1.9 %fusion.18 = bf16[6,96,301]{2,1,0:T(8,128)(2,1)} fusion(bf16[6,96,768]{2,1,0:T(8,128)(2,1)S(1)} %get-tuple-element.22, bf16[6,96,768]{2,1,0:T(8,128)(2,1)S(1)} %get-tuple-element.20, f32[768,301]{0,1:T(8,128)S(1)} %get-tuple-element.31, f32[768,301]{0,1:T(8,128)S(1)} %get-tuple-element.30), kind=kOutput, calls=%fused_computation.29 | convolution fusion | flops 537710400 | bytes 3965568 | tf_op jit(solution)/shard_map/while/body/eval_jaxpr/rgwk,kl->wrgl/dot_general | solution.py:67
  65.2 0.0 reduce-scatter.2.cloned.1.call-update
  65.2 0.0 copy-done.1
  65.2 11.2 %reduce-scatter.2.cloned.1.call-done = bf16[6,48,301]{2,1,0:T(8,128)(2,1)} async-done(((bf16[6,96,301]{2,1,0:T(8,128)(2,1)}), bf16[6,48,301]{2,1,0:T(8,128)(2,1)}) %reduce-scatter.2.cloned.1.call-update) | async-done | bytes 173392 | tf_op jit(solution)/shard_map/reduce_scatter | solution.py:95
  76.4 1.8 %convert_multiply_fusion = f32[6,48,301]{2,1,0:T(8,128)} fusion(bf16[6,48,301]{2,1,0:T(8,128)(2,1)} %reduce-scatter.2.cloned.1.call-done, f32[6,48]{1,0:T(8,128)S(1)} %convert_element_type.91), kind=kLoop, calls=%fused_computation.37 | loop fusion | flops 173376 | bytes 521280 | tf_op jit(solution)/shard_map/mul | solution.py:98
  (9 shorter events, 0.1 us)
Async XLA Ops:
  6.5 69.9 %reduce-scatter.2.cloned.1.call-start = ((), (), s32[]{:S(2)}) async-start(), calls=%async_computation.1 | async-start | bytes 663552 | tf_op jit(solution)/shard_map/reduce_scatter | solution.py:95
  6.6 25.5 %copy-start = (bf16[6,1,2048]{2,0,1:T(8,128)(2,1)S(1)}, bf16[6,1,2048]{2,0,1:T(8,128)(2,1)}, u32[]{:S(2)}) copy-start(bf16[6,1,2048]{2,0,1:T(8,128)(2,1)} %param.3) | copy-start | bytes 73732
  32.2 1.2 %copy-start.2 = (s32[6]{0:T(128)S(1)}, s32[6]{0:T(128)}, u32[]{:S(2)}) copy-start(s32[6]{0:T(128)} %param.4) | copy-start | bytes 76
  63.3 1.9 %copy-start.1 = (s32[6,48]{1,0:T(8,128)S(1)}, s32[6,48]{1,0:T(8,128)}, u32[]{:S(2)}) copy-start(s32[6,48]{1,0:T(8,128)} %param.5) | copy-start | bytes 3460
Sparse Core Ops, SparseCore 0:
  65.3 11.0 reduce-scatter.1
where the time goes:
time: 85.2 us; the launch traced here: 85 us
  other arithmetic  32 us (38%)
  blocking collectives  24.9 us (29%)
  between operations  13.5 us (16%)
  waiting for transfers between devices  11.2 us (13%)
  matrix products  2.82 us (3%)
    another operation x2, other arithmetic  25.9 us
    all_gather x1, blocking collectives, per_device(): incoming = lax.all_gather(whitened, 'chan', axis=0, tiled=True)  24.9 us
    reduce_scatter x1, waiting for transfers between devices, per_device(): lax.psum_scatter(placed.astype(jnp.float32).astype(jnp.bfloat16), 'tm', s...  11.2 us
    cos x1, other arithmetic, lag_table(): jnp.cos(angles)  3.74 us
    dot_general x1, matrix products, correlate(): jnp.einsum('rgwk,kl->wrgl', cross, lag_weights, preferred_element_type=jn...  1.86 us
    mul x1, other arithmetic, per_device(): return shares * pair_mask.astype(jnp.float32)[..., None]  1.8 us
  transfers between devices with their start and end apart: 1, of which 1 were waited for; matrix products, arithmetic and copies ran while one was open for 0% of the time, Pallas kernels for 0%

commit v1 on v0

--- a/solution.py
+++ b/solution.py
@@ -82,7 +82,14 @@
     whitened = whiten(samples, dead_flags, table_values)
     subwin = local_windows * lax.axis_size("tm")
     lag_weights = lag_table(length, F, LAGS, 1.0 / math.sqrt(subwin * F))
-    incoming = lax.all_gather(whitened, "chan", axis=0, tiled=True)
+    ways, here = (lax.axis_size("chan"), lax.axis_index("chan"))
+    incoming, reach = (whitened, 1)
+    while reach < ways:
+        theirs = lax.ppermute(incoming, "chan", [(d, d ^ reach) for d in range(ways)])
+        mine_first = jnp.concatenate([incoming, theirs], axis=0)
+        theirs_first = jnp.concatenate([theirs, incoming], axis=0)
+        incoming = jnp.where(here & reach == 0, mine_first, theirs_first)
+        reach = 2 * reach
     source_count = incoming.shape[0]
     group_size = pick_group(source_count, block_size * local_windows)
     grouped = incoming.reshape(source_count // group_size, group_size, local_windows, 2 * F)

time: 85.2 us -> 82.3 us (0.966)
  blocking collectives: 24.9 us -> 0 us
  waiting for transfers between devices: 11.2 us -> 25.5 us
  starting transfers between devices: 0.01 us -> 7.85 us
    all_gather x1 -> x0, blocking collectives: 24.9 us -> none  [per_device(): incoming = lax.all_gather(whitened, 'chan', axis=0, tiled=True)]
    ppermute x0 -> x4, waiting for transfers between devices: none -> 10.6 us  [per_device(): lax.ppermute(incoming, 'chan', [(d, d ^ reach) for d in range(ways)])]
    ppermute x0 -> x4, starting transfers between devices: none -> 7.85 us  [per_device(): lax.ppermute(incoming, 'chan', [(d, d ^ reach) for d in range(ways)])]
    reduce_scatter x1, waiting for transfers between devices: 11.2 us -> 15 us  [per_device(): lax.psum_scatter(placed.astype(jnp.float32).astype(jnp.bfloat16), 'tm', s...]
  transfers between devices with their start and end apart: 1 -> 5, of which waited for: 1 -> 4; matrix products, arithmetic and copies ran while one was open for 0% -> 5% of each run, Pallas kernels for 0% -> 0%
where the time goes in v1:
time: 82.3 us; the launch traced here: 82.1 us
  other arithmetic  32.3 us (39%)
  waiting for transfers between devices  25.5 us (31%)
  between operations  13.6 us (17%)
  starting transfers between devices  7.85 us (10%)
  matrix products  2.83 us (3%)
    another operation x2, other arithmetic  25.9 us
    reduce_scatter x1, waiting for transfers between devices, per_device(): lax.psum_scatter(placed.astype(jnp.float32).astype(jnp.bfloat16), 'tm', s...  15 us
    ppermute x4, waiting for transfers between devices, per_device(): lax.ppermute(incoming, 'chan', [(d, d ^ reach) for d in range(ways)])  10.6 us
    ppermute x4, starting transfers between devices, per_device(): lax.ppermute(incoming, 'chan', [(d, d ^ reach) for d in range(ways)])  7.85 us
    cos x1, other arithmetic, lag_table(): jnp.cos(angles)  3.73 us
    dot_general x1, matrix products, correlate(): jnp.einsum('rgwk,kl->wrgl', cross, lag_weights, preferred_element_type=jn...  1.87 us
    mul x1, other arithmetic, per_device(): return shares * pair_mask.astype(jnp.float32)[..., None]  1.8 us
  transfers between devices with their start and end apart: 5, of which 4 were waited for; matrix products, arithmetic and copies ran while one was open for 5% of the time, Pallas kernels for 0%

profile of v1, /device:TPU:0, one launch (start us, length us, event | category | flops | bytes accessed | tf_op | source)
XLA Modules:
  0.0 82.1 jit_solution(13820353604542867922)
XLA Ops:
  6.5 0.0 reduce-scatter.2.cloned.1.call-start
  6.5 0.1 multiply_subtract_fusion
  6.6 0.0 copy-start
  6.6 25.4 %cosine_convert_fusion = (bf16[2048,768]{1,0:T(8,128)(2,1)S(1)}, bf16[2048,768]{1,0:T(8,128)(2,1)S(1)}) fusion(s32[768]{0:T(1024)S(1)} %iota_add_fusion), kind=kLoop, calls=%fused_computation.11 | loop fusion | flops 26738688 | bytes 6294528 | tf_op jit(solution)/shard_map/convert.2
  32.1 0.0 copy-done
  32.1 0.1 convert_reduce_fusion
  32.2 0.0 copy-start.2
  32.2 1.0 %fusion.3 = f32[6,1536]{1,0:T(8,128)S(1)} fusion(bf16[2048,768]{1,0:T(8,128)(2,1)S(1)} %get-tuple-element.33, bf16[2048,768]{1,0:T(8,128)(2,1)S(1)} %get-tuple-element.32, bf16[6,1,2048]{2,0,1:T(8,128)(2,1)S(1)} %copy-done, f32[2048]{0:T(1024)S(1)} %multiply_subtract_fusion, f32[6]{0:T(128)S(1)} %broadcast_multiply_fusion.1), kind=kOutput, calls=%fused_computation.6 | convolution fusion | flops 50380800 | bytes 6361112 | tf_op jit(solution)/shard_map/dot_general | solution.py:39
  33.2 0.1 fusion.42
  33.3 0.1 slice_multiply_fusion.1
  33.4 0.0 copy-done.2
  33.4 0.1 fusion.43
  33.5 0.5 collective-permute-start
  34.0 0.1 fusion.33
  34.1 3.7 %fusion.27 = (f32[768,301]{0,1:T(8,128)S(1)}, f32[768,301]{0,1:T(8,128)S(1)}) fusion(s32[301]{0:T(512)S(1)} %iota_add_fusion.1, s32[768]{0:T(1024)S(1)} %iota_add_fusion), kind=kLoop, calls=%fused_computation.36 | loop fusion | flops 3467520 | bytes 1853620 | tf_op jit(solution)/shard_map/cos | solution.py:29
  37.9 0.0 collective-permute-done
  37.9 2.6 %collective-permute-start.1 = (bf16[12,1,1536]{2,0,1:T(8,128)(2,1)S(1)}, bf16[12,1,1536]{2,0,1:T(8,128)(2,1)S(1)}, u32[]{:S(2)}, u32[]{:S(2)}) collective-permute-start(bf16[12,1,1536]{2,0,1:T(8,128)(2,1)S(1)} %maximum_select_fusion.6), channel_id=1, source_target_pairs={{0,4},{2,6},{4,0},{6,2},{8,12},{10,14},{12,8},{14,10},{16,20},{18,... | collective-permute-start | bytes 110600 | tf_op jit(solution)/shard_map/ppermute | solution.py:88
  40.5 2.4 %collective-permute-done.1 = bf16[12,1,1536]{2,0,1:T(8,128)(2,1)S(1)} collective-permute-done((bf16[12,1,1536]{2,0,1:T(8,128)(2,1)S(1)}, bf16[12,1,1536]{2,0,1:T(8,128)(2,1)S(1)}, u32[]{:S(2)}, u32[]{:S(2)}) %collective-permute-start.1) | collective-permute-done | bytes 36896 | tf_op jit(solution)/shard_map/ppermute | solution.py:88
  42.9 1.9 %collective-permute-start.2 = (bf16[24,1,1536]{2,0,1:T(8,128)(2,1)S(1)}, bf16[24,1,1536]{2,0,1:T(8,128)(2,1)S(1)}, u32[]{:S(2)}, u32[]{:S(2)}) collective-permute-start(bf16[24,1,1536]{2,0,1:T(8,128)(2,1)S(1)} %maximum_select_fusion.4), channel_id=1, source_target_pairs={{0,8},{2,10},{4,12},{6,14},{8,0},{10,2},{12,4},{14,6},{16,24},{18,... | collective-permute-start | bytes 221192 | tf_op jit(solution)/shard_map/ppermute | solution.py:88
  44.8 2.5 %collective-permute-done.2 = bf16[24,1,1536]{2,0,1:T(8,128)(2,1)S(1)} collective-permute-done((bf16[24,1,1536]{2,0,1:T(8,128)(2,1)S(1)}, bf16[24,1,1536]{2,0,1:T(8,128)(2,1)S(1)}, u32[]{:S(2)}, u32[]{:S(2)}) %collective-permute-start.2) | collective-permute-done | bytes 73760 | tf_op jit(solution)/shard_map/ppermute | solution.py:88
  47.4 2.9 %collective-permute-start.3 = (bf16[48,1,1536]{2,0,1:T(8,128)(2,1)S(1)}, bf16[48,1,1536]{2,0,1:T(8,128)(2,1)S(1)}, u32[]{:S(2)}, u32[]{:S(2)}) collective-permute-start(bf16[48,1,1536]{2,0,1:T(8,128)(2,1)S(1)} %maximum_select_fusion.2), channel_id=1, source_target_pairs={{0,16},{2,18},{4,20},{6,22},{8,24},{10,26},{12,28},{14,30},{16,0},... | collective-permute-start | bytes 442376 | tf_op jit(solution)/shard_map/ppermute | solution.py:88
  50.3 5.7 %collective-permute-done.3 = bf16[48,1,1536]{2,0,1:T(8,128)(2,1)S(1)} collective-permute-done((bf16[48,1,1536]{2,0,1:T(8,128)(2,1)S(1)}, bf16[48,1,1536]{2,0,1:T(8,128)(2,1)S(1)}, u32[]{:S(2)}, u32[]{:S(2)}) %collective-permute-start.3) | collective-permute-done | bytes 147488 | tf_op jit(solution)/shard_map/ppermute | solution.py:88
  56.1 0.5 add_convert_fusion
  56.6 0.0 copy-start.1
  56.6 1.9 %fusion.18 = bf16[6,96,301]{2,1,0:T(8,128)(2,1)} fusion(bf16[6,96,768]{2,1,0:T(8,128)(2,1)S(1)} %get-tuple-element.22, bf16[6,96,768]{2,1,0:T(8,128)(2,1)S(1)} %get-tuple-element.20, f32[768,301]{0,1:T(8,128)S(1)} %get-tuple-element.31, f32[768,301]{0,1:T(8,128)S(1)} %get-tuple-element.30), kind=kOutput, calls=%fused_computation.29 | convolution fusion | flops 537710400 | bytes 3965568 | tf_op jit(solution)/shard_map/while/body/eval_jaxpr/rgwk,kl->wrgl/dot_general | solution.py:67
  58.5 0.0 reduce-scatter.2.cloned.1.call-update
  58.5 0.0 copy-done.1
  58.5 15.0 %reduce-scatter.2.cloned.1.call-done = bf16[6,48,301]{2,1,0:T(8,128)(2,1)} async-done(((bf16[6,96,301]{2,1,0:T(8,128)(2,1)}), bf16[6,48,301]{2,1,0:T(8,128)(2,1)}) %reduce-scatter.2.cloned.1.call-update) | async-done | bytes 173392 | tf_op jit(solution)/shard_map/reduce_scatter | solution.py:102
  73.5 1.8 %convert_multiply_fusion = f32[6,48,301]{2,1,0:T(8,128)} fusion(bf16[6,48,301]{2,1,0:T(8,128)(2,1)} %reduce-scatter.2.cloned.1.call-done, f32[6,48]{1,0:T(8,128)S(1)} %convert_element_type.111), kind=kLoop, calls=%fused_computation.37 | loop fusion | flops 173376 | bytes 521280 | tf_op jit(solution)/shard_map/mul | solution.py:105
  (15 shorter events, 0.3 us)
Async XLA Ops:
  6.5 66.9 %reduce-scatter.2.cloned.1.call-start = ((), (), s32[]{:S(2)}) async-start(), calls=%async_computation.1 | async-start | bytes 663552 | tf_op jit(solution)/shard_map/reduce_scatter | solution.py:102
  6.6 25.5 %copy-start = (bf16[6,1,2048]{2,0,1:T(8,128)(2,1)S(1)}, bf16[6,1,2048]{2,0,1:T(8,128)(2,1)}, u32[]{:S(2)}) copy-start(bf16[6,1,2048]{2,0,1:T(8,128)(2,1)} %param.3) | copy-start | bytes 73732
  32.2 1.2 %copy-start.2 = (s32[6]{0:T(128)S(1)}, s32[6]{0:T(128)}, u32[]{:S(2)}) copy-start(s32[6]{0:T(128)} %param.4) | copy-start | bytes 76
  33.5 4.4 %collective-permute-start = (bf16[6,1,1536]{2,0,1:T(8,128)(2,1)S(1)}, bf16[6,1,1536]{2,0,1:T(8,128)(2,1)S(1)}, u32[]{:S(2)}, u32[]{:S(2)}) collective-permute-start(bf16[6,1,1536]{2,0,1:T(8,128)(2,1)S(1)} %get-tuple-element.14), channel_id=1, source_target_pairs={{0,2},{2,0},{4,6},{6,4},{8,10},{10,8},{12,14},{14,12},{16,18},{18,... | collective-permute-start | bytes 55304 | tf_op jit(solution)/shard_map/ppermute | solution.py:88
  37.9 5.0 %collective-permute-start.1 = (bf16[12,1,1536]{2,0,1:T(8,128)(2,1)S(1)}, bf16[12,1,1536]{2,0,1:T(8,128)(2,1)S(1)}, u32[]{:S(2)}, u32[]{:S(2)}) collective-permute-start(bf16[12,1,1536]{2,0,1:T(8,128)(2,1)S(1)} %maximum_select_fusion.6), channel_id=1, source_target_pairs={{0,4},{2,6},{4,0},{6,2},{8,12},{10,14},{12,8},{14,10},{16,20},{18,... | collective-permute-start | bytes 110600 | tf_op jit(solution)/shard_map/ppermute | solution.py:88
  42.9 4.4 %collective-permute-start.2 = (bf16[24,1,1536]{2,0,1:T(8,128)(2,1)S(1)}, bf16[24,1,1536]{2,0,1:T(8,128)(2,1)S(1)}, u32[]{:S(2)}, u32[]{:S(2)}) collective-permute-start(bf16[24,1,1536]{2,0,1:T(8,128)(2,1)S(1)} %maximum_select_fusion.4), channel_id=1, source_target_pairs={{0,8},{2,10},{4,12},{6,14},{8,0},{10,2},{12,4},{14,6},{16,24},{18,... | collective-permute-start | bytes 221192 | tf_op jit(solution)/shard_map/ppermute | solution.py:88
  47.4 8.6 %collective-permute-start.3 = (bf16[48,1,1536]{2,0,1:T(8,128)(2,1)S(1)}, bf16[48,1,1536]{2,0,1:T(8,128)(2,1)S(1)}, u32[]{:S(2)}, u32[]{:S(2)}) collective-permute-start(bf16[48,1,1536]{2,0,1:T(8,128)(2,1)S(1)} %maximum_select_fusion.2), channel_id=1, source_target_pairs={{0,16},{2,18},{4,20},{6,22},{8,24},{10,26},{12,28},{14,30},{16,0},... | collective-permute-start | bytes 442376 | tf_op jit(solution)/shard_map/ppermute | solution.py:88
  56.6 1.9 %copy-start.1 = (s32[6,48]{1,0:T(8,128)S(1)}, s32[6,48]{1,0:T(8,128)}, u32[]{:S(2)}) copy-start(s32[6,48]{1,0:T(8,128)} %param.5) | copy-start | bytes 3460
Sparse Core Ops, SparseCore 0:
  58.6 14.8 reduce-scatter.1
